TPU v7x, 256 devices: a whole 4x4x8 slice. The times are simulated.
256 devices in a mesh: ctx: 32 (over x, z), head: 8 (over y, core).
Axes of the slice: x: 4, y: 4, z: 8, core: 2. Of those that a mesh axis runs over, the one named last changes fastest.
Arguments:
- queries: bfloat16 [8192, 32, 128], P('ctx', 'head'), may hold values from -40 to 40
- keys: bfloat16 [8192, 8, 128], P('ctx', 'head'), may hold values from -40 to 40
- values: bfloat16 [8192, 8, 128], P('ctx', 'head'), may hold values from -6 to 6
- doc_ids: int32 [8192], P('ctx'), may hold values from 0 to 3, never falling along the last dimension, each value on 1 to 4096 neighbouring positions
Outputs:
- attended: bfloat16 [8192, 4096], P(('ctx', 'head'))
Inputs may be any that keep to these rules, and one draw needn't show every extreme that they name: `doc_ids`: document numbers never fall along the sequence; each document has 1 to 4096 tokens and one has exactly 4096.
All inputs are finite; a program needn't handle non-finite values.
Results may differ from a plain program's by a relative error of at most 0.009.
Values may be sent and summed in bfloat16 or wider, within the bound.
No kernel may reach another device: no remote copies, remote signals or barrier semaphores. Data moves between devices by JAX's collectives and lax.ppermute only.
A program may use at most 128 MiB of HBM per device.

v0:
```python
import functools
import math

import jax
import jax.numpy as jnp
from jax import lax
from jax.experimental import pallas as pl
from jax.experimental.pallas import tpu as pltpu
from jax.sharding import Mesh
from jax.sharding import PartitionSpec as P


TOK = 256
D = 128
HEADS = 4
NZ = 8
NX = 4
HALF = 128
NEG = -1e30
PIECE = 2 * TOK + 8
NEAR = ((0, 0, 0, TOK, 0), (1, 0, 1, TOK, 2), (2, 0, 2, TOK, -2))
REST = (
    (0, 0, 0, TOK, 1),
    (0, PIECE, 0, PIECE + TOK, 3),
    (1, 0, 1, TOK, -1),
    (1, PIECE, 1, PIECE + TOK, -3),
    (2, 0, 3, 0, 4),
)
EVERY = NEAR + tuple((a + len(NEAR), i, b + len(NEAR), j, shift) for a, i, b, j, shift in REST)
MIB = 1 << 20
ROWS = TOK * HEADS
GROUPS = ROWS // HALF
SCALE = D**-0.5
SCALE2 = SCALE * math.log2(math.e)
VM = pl.BlockSpec(memory_space=pltpu.VMEM)


def prep_kernel(k_ref, v_ref, q_ref, ids_ref, kv_ref, qc_ref, ids, sems):
    copies = [
        pltpu.make_async_copy(ids_ref, ids, sems.at[0]),
        pltpu.make_async_copy(k_ref, kv_ref.at[0:TOK, :], sems.at[1]),
        pltpu.make_async_copy(v_ref, kv_ref.at[TOK : 2 * TOK, :], sems.at[2]),
        pltpu.make_async_copy(q_ref, qc_ref.at[0:ROWS, :], sems.at[3]),
    ]
    for copy in copies:
        copy.start()
    copies[0].wait()
    row = lax.broadcasted_iota(jnp.int32, (8, D), 0)
    cnt = jnp.zeros((8, D), jnp.float32)
    for d in (1, 2, 3):
        n = jnp.sum(jnp.where(ids[...] < d, 1.0, 0.0))
        cnt = jnp.where(row == d, n, cnt)
    cnt = cnt.astype(jnp.bfloat16)
    kv_ref[2 * TOK : PIECE, :] = cnt
    qc_ref[ROWS : ROWS + 8, :] = cnt
    for copy in copies[1:]:
        copy.wait()


def prep(*args):
    args = [pltpu.with_memory_space_constraint(a, pltpu.HBM) for a in args]
    return pl.pallas_call(
        prep_kernel,
        out_shape=[
            jax.ShapeDtypeStruct((PIECE, D), jnp.bfloat16),
            jax.ShapeDtypeStruct((ROWS + 8, D), jnp.bfloat16),
        ],
        in_specs=[pl.BlockSpec(memory_space=pltpu.HBM)] * 4,
        out_specs=[VM] * 2,
        scratch_shapes=[pltpu.VMEM((2, D), jnp.int32), pltpu.SemaphoreType.DMA((4,))],
        compiler_params=pltpu.CompilerParams(vmem_limit_bytes=4 * MIB),
    )(*args)


def attn_kernel(deltas, blocks, merge, last, *refs):
    n, nb = len(deltas), len(blocks)
    arrays = 1 + max(max(block[0], block[2]) for block in blocks)
    kv, refs = refs[:arrays], refs[arrays:]
    qs, refs = refs[:n], refs[n:]
    before, refs = (refs[: 3 * n], refs[3 * n :]) if merge else (None, refs)
    per = {"state": 3, "send": 1, "keep": 2}[last]
    outs, (kscr, vscr, sscr, acc, mscr, lscr, rows_scr, cscr) = refs[: per * n], refs[per * n :]
    x, z = lax.axis_index("x"), lax.axis_index("z")
    for i, (k_at, k_row, v_at, v_row, shift) in enumerate(blocks):
        kscr[i] = kv[k_at][k_row : k_row + TOK, :]
        vscr[i] = kv[v_at][v_row : v_row + TOK, :]
        cnt = kv[v_at][v_row + TOK : v_row + TOK + 8, :].astype(jnp.float32)
        cscr[i, 0] = lax.rem(z - shift + NZ, NZ)
        for d in (1, 2, 3):
            cscr[i, d] = jnp.max(cnt[d : d + 1, :]).astype(jnp.int32)

    for j, delta in enumerate(deltas):
        q_ref = qs[j]
        cnt = q_ref[ROWS : ROWS + 8, :].astype(jnp.float32)
        ends = [jnp.max(cnt[d : d + 1, :]).astype(jnp.int32) for d in (1, 2, 3)]

        def pick(tok, a, b, c, d, ends=ends):
            return jnp.where(
                tok >= ends[2], d, jnp.where(tok >= ends[1], c, jnp.where(tok >= ends[0], b, a))
            )

        def bounds(i, tok, delta=delta, pick=pick):
            c1, c2, c3 = cscr[i, 1], cscr[i, 2], cscr[i, 3]
            lo = pick(tok, jnp.int32(0), c1, c2, c3)
            hi = pick(tok, c1, c2, c3, jnp.int32(TOK))
            if delta == 0:
                b = cscr[i, 0]
                hi = jnp.minimum(hi, jnp.where(b < z, TOK, jnp.where(b == z, tok + 1, 0)))
            else:
                hi = jnp.where(x + delta < NX, hi, 0)
            return lo, hi

        def state(i, bounds=bounds):
            lo_a, hi_a = bounds(i, 0)
            lo_b, hi_b = bounds(i, TOK - 1)
            seen = hi_b > lo_a
            whole = (lo_b <= 0) & (hi_a >= TOK)
            return jnp.where(seen, jnp.where(whole, 2, 1), 0)

        def scores(masked, i, q_ref=q_ref, bounds=bounds):
            s = lax.dot_general(
                q_ref[0:ROWS, :],
                kscr[i],
                (((1,), (1,)), ((), ())),
                preferred_element_type=jnp.float32,
            )
            if masked:
                tok = lax.broadcasted_iota(jnp.int32, (ROWS, D), 0) >> 2
                pos = lax.broadcasted_iota(jnp.int32, (ROWS, D), 1)
                lo, hi = bounds(i, tok)
                halves = [
                    jnp.where((pos + c >= lo) & (pos + c < hi), s[:, c : c + D], NEG)
                    for c in range(0, TOK, D)
                ]
                s = jnp.concatenate(halves, axis=1)
            sscr[i] = s
            mscr[...] = jnp.maximum(mscr[...], jnp.maximum(s[:, 0:D], s[:, D : 2 * D]))

        def first_pass(i, _, state=state, scores=scores):
            st = state(i)
            pl.when(st == 1)(lambda: scores(True, i))
            pl.when(st == 2)(lambda: scores(False, i))
            return 0

        mscr[...] = before[3 * j + 1][...] if merge else jnp.full((ROWS, D), NEG, jnp.float32)
        lax.fori_loop(0, nb, first_pass, 0)
        m = jnp.max(mscr[...], axis=1, keepdims=True)
        if merge:
            shrink = jnp.exp2((before[3 * j + 1][...] - m) * SCALE2)
            acc[...] = before[3 * j][...] * shrink
            lscr[...] = before[3 * j + 2][...] * shrink
        else:
            acc[...] = jnp.zeros_like(acc)
            lscr[...] = jnp.zeros_like(lscr)
        mscr[...] = jnp.broadcast_to(m, (ROWS, D))

        def weigh(i):
            s = sscr[i]
            top = mscr[...]
            lo = jnp.exp2((s[:, 0:D] - top) * SCALE2)
            hi = jnp.exp2((s[:, D : 2 * D] - top) * SCALE2)
            lscr[...] += lo + hi
            p = jnp.concatenate([lo.astype(jnp.bfloat16), hi.astype(jnp.bfloat16)], axis=1)
            acc[...] += jnp.dot(p, vscr[i], preferred_element_type=jnp.float32)

        def second_pass(i, _, state=state):
            pl.when(state(i) > 0)(lambda: weigh(i))
            return 0

        lax.fori_loop(0, nb, second_pass, 0)
        if last == "state":
            outs[3 * j][...] = acc[...]
            outs[3 * j + 1][...] = mscr[...]
            outs[3 * j + 2][...] = lscr[...]
            continue
        total = jnp.maximum(jnp.sum(lscr[...], axis=1, keepdims=True), 1e-30)
        outs[per * j][0:ROWS, :] = (acc[...] * (1.0 / total)).astype(outs[per * j].dtype)
        lse = jnp.broadcast_to(m * SCALE + jnp.log(total), (ROWS, D))
        for g in range(GROUPS):
            rows_scr[g : g + 1, :] = lse[g * HALF : (g + 1) * HALF, :].T[0:1, :]
        if last == "keep":
            outs[2 * j + 1][...] = rows_scr[...]
        elif last == "send":
            rest = rows_scr[...]
            for t in range(3):
                part = rest.astype(jnp.bfloat16)
                outs[j][ROWS + t * GROUPS : ROWS + (t + 1) * GROUPS, :] = part
                rest = rest - part.astype(jnp.float32)


def attn(deltas, blocks, kv, qs, before, last):
    n, nb = len(deltas), len(blocks)
    args = (*kv, *qs, *before)
    wide = jax.ShapeDtypeStruct((ROWS, D), jnp.float32)
    outs = {
        "state": [wide] * 3,
        "send": [jax.ShapeDtypeStruct((ROWS + 3 * GROUPS, D), jnp.bfloat16)],
        "keep": [wide, jax.ShapeDtypeStruct((GROUPS, D), jnp.float32)],
    }[last] * n
    return pl.pallas_call(
        functools.partial(attn_kernel, deltas, blocks, bool(before), last),
        out_shape=outs,
        in_specs=[VM] * len(args),
        out_specs=[VM] * len(outs),
        scratch_shapes=[
            pltpu.VMEM((nb, TOK, D), jnp.bfloat16),
            pltpu.VMEM((nb, TOK, D), jnp.bfloat16),
            pltpu.VMEM((nb, ROWS, TOK), jnp.float32),
            pltpu.VMEM((ROWS, D), jnp.float32),
            pltpu.VMEM((ROWS, D), jnp.float32),
            pltpu.VMEM((ROWS, D), jnp.float32),
            pltpu.VMEM((GROUPS, D), jnp.float32),
            pltpu.SMEM((nb, 4), jnp.int32),
        ],
        compiler_params=pltpu.CompilerParams(vmem_limit_bytes=20 * MIB),
        cost_estimate=pl.CostEstimate(
            flops=4 * ROWS * D * TOK * nb * n,
            bytes_accessed=MIB,
            transcendentals=ROWS * TOK * nb * n,
        ),
    )(*args)


def combine_kernel(a_ref, lse_ref, b_ref, c_ref, o_ref, scr):
    x = lax.axis_index("x")

    def lse_of(ref, delta):
        terms = [
            ref[ROWS + t * GROUPS : ROWS + (t + 1) * GROUPS, :].astype(jnp.float32)
            for t in range(3)
        ]
        return jnp.where(x >= delta, terms[0] + (terms[1] + terms[2]), NEG)

    lses = (lse_ref[...], lse_of(b_ref, 1), lse_of(c_ref, 2))
    top = jnp.maximum(jnp.maximum(lses[0], lses[1]), lses[2])
    ws = [jnp.exp(lse - top) for lse in lses]
    inv = 1.0 / (ws[0] + ws[1] + ws[2])
    pad = jnp.zeros((HALF - GROUPS, D), jnp.float32)
    ws = [jnp.concatenate([w * inv, pad], axis=0).T for w in ws]
    for g in range(GROUPS):
        rows = slice(g * HALF, (g + 1) * HALF)
        scr[rows, :] = sum(
            ref[rows, :].astype(jnp.float32) * w[:, g : g + 1]
            for ref, w in zip((a_ref, b_ref, c_ref), ws)
        )
    for h in range(HEADS):
        rows = pl.ds(h, TOK, stride=HEADS)
        o_ref[:, h * D : (h + 1) * D] = scr[rows, :].astype(o_ref.dtype)


def combine(*args):
    return pl.pallas_call(
        combine_kernel,
        out_shape=jax.ShapeDtypeStruct((TOK, HEADS * D), jnp.bfloat16),
        in_specs=[VM] * len(args),
        out_specs=VM,
        scratch_shapes=[pltpu.VMEM((ROWS, D), jnp.float32)],
        compiler_params=pltpu.CompilerParams(vmem_limit_bytes=6 * MIB),
    )(*args)


def along(a, axis, shift, n):
    pairs = [(i, i + shift) for i in range(n)]
    if axis == "x":
        pairs = [(i, j) for i, j in pairs if 0 <= j < n]
    return lax.ppermute(a, axis, [(i, j % n) for i, j in pairs])


def local(queries, keys, values, doc_ids):
    kv, q = prep(
        keys.reshape(TOK, D), values.reshape(TOK, D), queries.reshape(ROWS, D), doc_ids.reshape(2, D)
    )
    up2 = along(kv, "z", 2, NZ)
    dn2 = along(kv, "z", -2, NZ)
    q2 = along(q, "x", -2, NX)
    q1 = along(q, "x", -1, NX)
    up13 = along(jnp.concatenate([kv, up2], axis=0), "z", 1, NZ)
    dn13 = along(jnp.concatenate([kv, dn2], axis=0), "z", -1, NZ)
    far_k = along(up2[0:TOK], "z", 2, NZ)
    far_v = along(dn2[TOK:PIECE], "z", -2, NZ)
    first, rest = [kv, up2, dn2], [up13, dn13, far_k, far_v]
    near1 = attn((1,), NEAR, first, [q1], (), "state")
    near2 = attn((2,), NEAR, first, [q2], (), "state")
    (o1,) = attn((1,), REST, rest, [q1], near1, "send")
    r1 = along(o1, "x", 1, NX)
    (o2,) = attn((2,), REST, rest, [q2], near2, "send")
    r2 = along(o2, "x", 2, NX)
    o0, lse0 = attn((0,), EVERY, first + rest, [q], (), "keep")
    merged = combine(o0, lse0, r1, r2)
    return lax.all_to_all(merged, ("y", "core"), split_axis=0, concat_axis=1, tiled=True)


def solution(mesh):
    grid = Mesh(mesh.devices.reshape(NX, NZ, 4, 2), ("x", "z", "y", "core"))
    ctx, head = ("x", "z"), ("y", "core")
    return jax.shard_map(
        local,
        mesh=grid,
        in_specs=(P(ctx, head, None), P(ctx, head, None), P(ctx, head, None), P(ctx)),
        out_specs=P(ctx + head, None),
        check_vma=False,
    )
```

profile of v0, /device:TPU:4, one launch (start us, length us, event | category | flops | bytes accessed | tf_op | source)
XLA Modules:
  0.0 59.0 jit_solution(17156541057320753508)
XLA Ops:
  0.0 1.1 %shard_map.46 = (bf16[520,128]{1,0:T(8,128)(2,1)S(1)}, bf16[1032,128]{1,0:T(8,128)(2,1)S(1)}) custom-call(bf16[256,128]{1,0:T(8,128)(2,1)} %bitcast.11, bf16[256,128]{1,0:T(8,128)(2,1)} %bitcast.12, bf16[1024,128]{1,0:T(8,128)(2,1)} %bitcast.10, s32[2,128]{1,0:T(2,128)} %bitcast.13), custom_call_target="tpu_custom_call" | custom-call | tf_op jit(solution)/shard_map/pallas_call | solution.py:62
  1.1 3.3 %collective-permute-start = (bf16[520,128]{1,0:T(8,128)(2,1)S(1)}, bf16[520,128]{1,0:T(8,128)(2,1)S(1)}, u32[]{:S(2)}, u32[]{:S(2)}) collective-permute-start(bf16[520,128]{1,0:T(8,128)(2,1)S(1)} %get-tuple-element.15.refs_0_), channel_id=1, source_target_pairs={{0,16},{8,24},{16,32},{24,40},{32,48},{40,56},{48,0},{56,8},{1,17}... | collective-permute-start | bytes 399368 | tf_op jit(solution)/shard_map/ppermute | solution.py:266
  4.4 3.1 %collective-permute-start.1 = (bf16[520,128]{1,0:T(8,128)(2,1)S(1)}, bf16[520,128]{1,0:T(8,128)(2,1)S(1)}, u32[]{:S(2)}, u32[]{:S(2)}) collective-permute-start(bf16[520,128]{1,0:T(8,128)(2,1)S(1)} %get-tuple-element.15.refs_0_), channel_id=1, source_target_pairs={{0,48},{8,56},{16,0},{24,8},{32,16},{40,24},{48,32},{56,40},{1,49}... | collective-permute-start | bytes 399368 | tf_op jit(solution)/shard_map/ppermute | solution.py:266
  7.6 2.4 %collective-permute-start.8 = (bf16[1032,128]{1,0:T(8,128)(2,1)S(1)}, bf16[1032,128]{1,0:T(8,128)(2,1)S(1)}, u32[]{:S(2)}, u32[]{:S(2)}) collective-permute-start(bf16[1032,128]{1,0:T(8,128)(2,1)S(1)} %get-tuple-element.16.refs_7_), channel_id=1, source_target_pairs={{128,0},{192,64},{129,1},{193,65},{130,2},{194,66},{131,3},{195,67... | collective-permute-start | bytes 792584 | tf_op jit(solution)/shard_map/ppermute | solution.py:266
  10.0 1.9 %collective-permute-start.6 = (bf16[1032,128]{1,0:T(8,128)(2,1)S(1)}, bf16[1032,128]{1,0:T(8,128)(2,1)S(1)}, u32[]{:S(2)}, u32[]{:S(2)}) collective-permute-start(bf16[1032,128]{1,0:T(8,128)(2,1)S(1)} %get-tuple-element.16.refs_7_), channel_id=1, source_target_pairs={{64,0},{128,64},{192,128},{65,1},{129,65},{193,129},{66,2},{130,66... | collective-permute-start | bytes 792584 | tf_op jit(solution)/shard_map/ppermute | solution.py:266
  11.9 0.0 collective-permute-done.refs_1_
  11.9 3.1 %collective-permute-done.1.refs_2_ = bf16[520,128]{1,0:T(8,128)(2,1)S(1)} collective-permute-done((bf16[520,128]{1,0:T(8,128)(2,1)S(1)}, bf16[520,128]{1,0:T(8,128)(2,1)S(1)}, u32[]{:S(2)}, u32[]{:S(2)}) %collective-permute-start.1) | collective-permute-done | bytes 133152 | tf_op jit(solution)/shard_map/ppermute | solution.py:266
  15.0 0.1 pad_maximum_fusion
  15.1 0.1 collective-permute-start.2
  15.2 3.2 %collective-permute-start.3 = (bf16[1040,128]{1,0:T(8,128)(2,1)S(1)}, bf16[1040,128]{1,0:T(8,128)(2,1)S(1)}, u32[]{:S(2)}, u32[]{:S(2)}) collective-permute-start(bf16[1040,128]{1,0:T(8,128)(2,1)S(1)} %get-tuple-element.25), channel_id=1, source_target_pairs={{0,56},{8,0},{16,8},{24,16},{32,24},{40,32},{48,40},{56,48},{1,57}... | collective-permute-start | bytes 798728 | tf_op jit(solution)/shard_map/ppermute | solution.py:266
  18.4 1.6 %collective-permute-start.5 = (bf16[264,128]{1,0:T(8,128)(2,1)S(1)}, bf16[264,128]{1,0:T(8,128)(2,1)S(1)}, u32[]{:S(2)}, u32[]{:S(2)}) collective-permute-start(bf16[264,128]{1,0:T(8,128)(2,1)S(1)} %slice.9), channel_id=1, source_target_pairs={{0,48},{8,56},{16,0},{24,8},{32,16},{40,24},{48,32},{56,40},{1,49}... | collective-permute-start | bytes 202760 | tf_op jit(solution)/shard_map/ppermute | solution.py:266
  20.0 0.0 collective-permute-done.8.refs_3_.refs_4_
  20.0 1.4 %collective-permute-start.4 = (bf16[256,128]{1,0:T(8,128)(2,1)S(1)}, bf16[256,128]{1,0:T(8,128)(2,1)S(1)}, u32[]{:S(2)}, u32[]{:S(2)}) collective-permute-start(bf16[256,128]{1,0:T(8,128)(2,1)S(1)} %slice.8), channel_id=1, source_target_pairs={{0,16},{8,24},{16,32},{24,40},{32,48},{40,56},{48,0},{56,8},{1,17}... | collective-permute-start | bytes 196616 | tf_op jit(solution)/shard_map/ppermute | solution.py:266
  21.4 0.6 %shard_map.50 = (f32[1024,128]{1,0:T(8,128)S(1)}, f32[1024,128]{1,0:T(8,128)S(1)}, f32[1024,128]{1,0:T(8,128)S(1)}) custom-call(bf16[520,128]{1,0:T(8,128)(2,1)S(1)} %get-tuple-element.15.refs_0_, bf16[520,128]{1,0:T(8,128)(2,1)S(1)} %collective-permute-done.refs_1_, bf16[520,128]{1,0:T(8,128)(2,1)S(1)} %collective-permute-done.1.refs_2_, ...), custom_call_target="tpu_custom_call" | custom-call | flops 402653184 | bytes 1048576 | tf_op jit(solution)/shard_map/pallas_call | solution.py:200
  22.0 1.5 %collective-permute-done.6.refs_3_.refs_4_ = bf16[1032,128]{1,0:T(8,128)(2,1)S(1)} collective-permute-done((bf16[1032,128]{1,0:T(8,128)(2,1)S(1)}, bf16[1032,128]{1,0:T(8,128)(2,1)S(1)}, u32[]{:S(2)}, u32[]{:S(2)}) %collective-permute-start.6) | collective-permute-done | bytes 264224 | tf_op jit(solution)/shard_map/ppermute | solution.py:266
  23.5 2.4 %shard_map.48 = (f32[1024,128]{1,0:T(8,128)S(1)}, f32[1024,128]{1,0:T(8,128)S(1)}, f32[1024,128]{1,0:T(8,128)S(1)}) custom-call(bf16[520,128]{1,0:T(8,128)(2,1)S(1)} %get-tuple-element.15.refs_0_, bf16[520,128]{1,0:T(8,128)(2,1)S(1)} %collective-permute-done.refs_1_, bf16[520,128]{1,0:T(8,128)(2,1)S(1)} %collective-permute-done.1.refs_2_, ...), custom_call_target="tpu_custom_call" | custom-call | flops 402653184 | bytes 1048576 | tf_op jit(solution)/shard_map/pallas_call | solution.py:200
  26.0 0.5 collective-permute-done.4.refs_5_.refs_2_
  26.4 2.7 %collective-permute-done.5.refs_6_.refs_3_ = bf16[264,128]{1,0:T(8,128)(2,1)S(1)} collective-permute-done((bf16[264,128]{1,0:T(8,128)(2,1)S(1)}, bf16[264,128]{1,0:T(8,128)(2,1)S(1)}, u32[]{:S(2)}, u32[]{:S(2)}) %collective-permute-start.5) | collective-permute-done | bytes 67616 | tf_op jit(solution)/shard_map/ppermute | solution.py:266
  29.1 0.0 collective-permute-done.2.refs_3_.refs_0_
  29.1 0.0 collective-permute-done.3.refs_4_.refs_1_
  29.1 1.0 %shard_map.51 = bf16[1048,128]{1,0:T(8,128)(2,1)S(1)} custom-call(bf16[1040,128]{1,0:T(8,128)(2,1)S(1)} %collective-permute-done.2.refs_3_.refs_0_, bf16[1040,128]{1,0:T(8,128)(2,1)S(1)} %collective-permute-done.3.refs_4_.refs_1_, bf16[256,128]{1,0:T(8,128)(2,1)S(1)} %collective-permute-done.4.refs_5_.refs_2_, ...), custom_call_target="tpu_custom_call" | custom-call | flops 671088640 | bytes 1048576 | tf_op jit(solution)/shard_map/pallas_call | solution.py:200
  30.1 1.3 %collective-permute-start.9 = (bf16[1048,128]{1,0:T(8,128)(2,1)S(1)}, bf16[1048,128]{1,0:T(8,128)(2,1)S(1)}, u32[]{:S(2)}, u32[]{:S(2)}) collective-permute-start(bf16[1048,128]{1,0:T(8,128)(2,1)S(1)} %shard_map.51), channel_id=1, source_target_pairs={{0,128},{64,192},{1,129},{65,193},{2,130},{66,194},{3,131},{67,195... | collective-permute-start | bytes 804872 | tf_op jit(solution)/shard_map/ppermute | solution.py:266
  31.4 4.0 %shard_map.49 = bf16[1048,128]{1,0:T(8,128)(2,1)S(1)} custom-call(bf16[1040,128]{1,0:T(8,128)(2,1)S(1)} %collective-permute-done.2.refs_3_.refs_0_, bf16[1040,128]{1,0:T(8,128)(2,1)S(1)} %collective-permute-done.3.refs_4_.refs_1_, bf16[256,128]{1,0:T(8,128)(2,1)S(1)} %collective-permute-done.4.refs_5_.refs_2_, ...), custom_call_target="tpu_custom_call" | custom-call | flops 671088640 | bytes 1048576 | tf_op jit(solution)/shard_map/pallas_call | solution.py:200
  35.4 1.9 %collective-permute-start.7 = (bf16[1048,128]{1,0:T(8,128)(2,1)S(1)}, bf16[1048,128]{1,0:T(8,128)(2,1)S(1)}, u32[]{:S(2)}, u32[]{:S(2)}) collective-permute-start(bf16[1048,128]{1,0:T(8,128)(2,1)S(1)} %shard_map.49), channel_id=1, source_target_pairs={{0,64},{64,128},{128,192},{1,65},{65,129},{129,193},{2,66},{66,130... | collective-permute-start | bytes 804872 | tf_op jit(solution)/shard_map/ppermute | solution.py:266
  37.3 2.1 %shard_map.47 = (f32[1024,128]{1,0:T(8,128)S(1)}, f32[8,128]{1,0:T(8,128)S(1)}) custom-call(bf16[520,128]{1,0:T(8,128)(2,1)S(1)} %get-tuple-element.15.refs_0_, bf16[520,128]{1,0:T(8,128)(2,1)S(1)} %collective-permute-done.refs_1_, bf16[520,128]{1,0:T(8,128)(2,1)S(1)} %collective-permute-done.1.refs_2_, ...), custom_call_target="tpu_custom_call" | custom-call | flops 1073741824 | bytes 1048576 | tf_op jit(solution)/shard_map/pallas_call | solution.py:200
  39.5 3.1 %collective-permute-done.9.c_ref = bf16[1048,128]{1,0:T(8,128)(2,1)S(1)} collective-permute-done((bf16[1048,128]{1,0:T(8,128)(2,1)S(1)}, bf16[1048,128]{1,0:T(8,128)(2,1)S(1)}, u32[]{:S(2)}, u32[]{:S(2)}) %collective-permute-start.9) | collective-permute-done | bytes 268320 | tf_op jit(solution)/shard_map/ppermute | solution.py:266
  42.5 3.2 %collective-permute-done.7.b_ref = bf16[1048,128]{1,0:T(8,128)(2,1)S(1)} collective-permute-done((bf16[1048,128]{1,0:T(8,128)(2,1)S(1)}, bf16[1048,128]{1,0:T(8,128)(2,1)S(1)}, u32[]{:S(2)}, u32[]{:S(2)}) %collective-permute-start.7) | collective-permute-done | bytes 268320 | tf_op jit(solution)/shard_map/ppermute | solution.py:266
  45.8 0.7 %shard_map.52 = bf16[256,512]{1,0:T(8,128)(2,1)S(1)} custom-call(f32[1024,128]{1,0:T(8,128)S(1)} %get-tuple-element.17.a_ref, f32[8,128]{1,0:T(8,128)S(1)} %get-tuple-element.18.lse_ref, bf16[1048,128]{1,0:T(8,128)(2,1)S(1)} %collective-permute-done.7.b_ref, bf16[1048,128]{1,0:T(8,128)(2,1)S(1)} %collective-permute-done.9.c_ref), custom_call_target="tpu_custom_call" | custom-call | tf_op jit(solution)/shard_map/pallas_call | solution.py:252
  46.5 11.8 %all_to_all.19 = bf16[8,32,512]{2,1,0:T(8,128)(2,1)S(1)} all-to-all(bf16[8,32,512]{2,1,0:T(8,128)(2,1)S(1)} %bitcast.8), channel_id=1, replica_groups=mesh['x'=4,'z'=8,'y'=4,'core'=2] {'y','core'}, dimensions={0} | all-to-all | bytes 524288 | tf_op jit(solution)/shard_map/all_to_all | solution.py:290
  58.3 0.7 %copy.6 = bf16[8,4,8,512]{3,2,0,1:T(8,128)(2,1)} copy(bf16[8,4,8,512]{3,2,1,0:T(8,128)(2,1)S(1)} %bitcast.9) | data formatting | bytes 524288 | tf_op jit(solution)/shard_map/all_to_all | solution.py:290
  (2 shorter events, 0.0 us)
Async XLA Ops:
  1.1 10.8 %collective-permute-start = (bf16[520,128]{1,0:T(8,128)(2,1)S(1)}, bf16[520,128]{1,0:T(8,128)(2,1)S(1)}, u32[]{:S(2)}, u32[]{:S(2)}) collective-permute-start(bf16[520,128]{1,0:T(8,128)(2,1)S(1)} %get-tuple-element.15.refs_0_), channel_id=1, source_target_pairs={{0,16},{8,24},{16,32},{24,40},{32,48},{40,56},{48,0},{56,8},{1,17}... | collective-permute-start | bytes 399368 | tf_op jit(solution)/shard_map/ppermute | solution.py:266
  4.4 10.6 %collective-permute-start.1 = (bf16[520,128]{1,0:T(8,128)(2,1)S(1)}, bf16[520,128]{1,0:T(8,128)(2,1)S(1)}, u32[]{:S(2)}, u32[]{:S(2)}) collective-permute-start(bf16[520,128]{1,0:T(8,128)(2,1)S(1)} %get-tuple-element.15.refs_0_), channel_id=1, source_target_pairs={{0,48},{8,56},{16,0},{24,8},{32,16},{40,24},{48,32},{56,40},{1,49}... | collective-permute-start | bytes 399368 | tf_op jit(solution)/shard_map/ppermute | solution.py:266
  7.6 12.4 %collective-permute-start.8 = (bf16[1032,128]{1,0:T(8,128)(2,1)S(1)}, bf16[1032,128]{1,0:T(8,128)(2,1)S(1)}, u32[]{:S(2)}, u32[]{:S(2)}) collective-permute-start(bf16[1032,128]{1,0:T(8,128)(2,1)S(1)} %get-tuple-element.16.refs_7_), channel_id=1, source_target_pairs={{128,0},{192,64},{129,1},{193,65},{130,2},{194,66},{131,3},{195,67... | collective-permute-start | bytes 792584 | tf_op jit(solution)/shard_map/ppermute | solution.py:266
  10.0 13.6 %collective-permute-start.6 = (bf16[1032,128]{1,0:T(8,128)(2,1)S(1)}, bf16[1032,128]{1,0:T(8,128)(2,1)S(1)}, u32[]{:S(2)}, u32[]{:S(2)}) collective-permute-start(bf16[1032,128]{1,0:T(8,128)(2,1)S(1)} %get-tuple-element.16.refs_7_), channel_id=1, source_target_pairs={{64,0},{128,64},{192,128},{65,1},{129,65},{193,129},{66,2},{130,66... | collective-permute-start | bytes 792584 | tf_op jit(solution)/shard_map/ppermute | solution.py:266
  15.1 14.0 %collective-permute-start.2 = (bf16[1040,128]{1,0:T(8,128)(2,1)S(1)}, bf16[1040,128]{1,0:T(8,128)(2,1)S(1)}, u32[]{:S(2)}, u32[]{:S(2)}) collective-permute-start(bf16[1040,128]{1,0:T(8,128)(2,1)S(1)} %get-tuple-element.26), channel_id=1, source_target_pairs={{0,8},{8,16},{16,24},{24,32},{32,40},{40,48},{48,56},{56,0},{1,9},... | collective-permute-start | bytes 798728 | tf_op jit(solution)/shard_map/ppermute | solution.py:266
  15.2 13.9 %collective-permute-start.3 = (bf16[1040,128]{1,0:T(8,128)(2,1)S(1)}, bf16[1040,128]{1,0:T(8,128)(2,1)S(1)}, u32[]{:S(2)}, u32[]{:S(2)}) collective-permute-start(bf16[1040,128]{1,0:T(8,128)(2,1)S(1)} %get-tuple-element.25), channel_id=1, source_target_pairs={{0,56},{8,0},{16,8},{24,16},{32,24},{40,32},{48,40},{56,48},{1,57}... | collective-permute-start | bytes 798728 | tf_op jit(solution)/shard_map/ppermute | solution.py:266
  18.4 10.7 %collective-permute-start.5 = (bf16[264,128]{1,0:T(8,128)(2,1)S(1)}, bf16[264,128]{1,0:T(8,128)(2,1)S(1)}, u32[]{:S(2)}, u32[]{:S(2)}) collective-permute-start(bf16[264,128]{1,0:T(8,128)(2,1)S(1)} %slice.9), channel_id=1, source_target_pairs={{0,48},{8,56},{16,0},{24,8},{32,16},{40,24},{48,32},{56,40},{1,49}... | collective-permute-start | bytes 202760 | tf_op jit(solution)/shard_map/ppermute | solution.py:266
  20.0 6.5 %collective-permute-start.4 = (bf16[256,128]{1,0:T(8,128)(2,1)S(1)}, bf16[256,128]{1,0:T(8,128)(2,1)S(1)}, u32[]{:S(2)}, u32[]{:S(2)}) collective-permute-start(bf16[256,128]{1,0:T(8,128)(2,1)S(1)} %slice.8), channel_id=1, source_target_pairs={{0,16},{8,24},{16,32},{24,40},{32,48},{40,56},{48,0},{56,8},{1,17}... | collective-permute-start | bytes 196616 | tf_op jit(solution)/shard_map/ppermute | solution.py:266
  30.1 12.5 %collective-permute-start.9 = (bf16[1048,128]{1,0:T(8,128)(2,1)S(1)}, bf16[1048,128]{1,0:T(8,128)(2,1)S(1)}, u32[]{:S(2)}, u32[]{:S(2)}) collective-permute-start(bf16[1048,128]{1,0:T(8,128)(2,1)S(1)} %shard_map.51), channel_id=1, source_target_pairs={{0,128},{64,192},{1,129},{65,193},{2,130},{66,194},{3,131},{67,195... | collective-permute-start | bytes 804872 | tf_op jit(solution)/shard_map/ppermute | solution.py:266
  35.4 10.4 %collective-permute-start.7 = (bf16[1048,128]{1,0:T(8,128)(2,1)S(1)}, bf16[1048,128]{1,0:T(8,128)(2,1)S(1)}, u32[]{:S(2)}, u32[]{:S(2)}) collective-permute-start(bf16[1048,128]{1,0:T(8,128)(2,1)S(1)} %shard_map.49), channel_id=1, source_target_pairs={{0,64},{64,128},{128,192},{1,65},{65,129},{129,193},{2,66},{66,130... | collective-permute-start | bytes 804872 | tf_op jit(solution)/shard_map/ppermute | solution.py:266
where the time goes:
time: 59.2 us; the launch traced here: 59 us
  starting transfers between devices  20.3 us (34%)
  waiting for transfers between devices  14.1 us (24%)
  Pallas kernels  12 us (20%)
  blocking collectives  11.8 us (20%)
  local copies, waits for them, and re-layouts  0.73 us (1%)
    ppermute x10, starting transfers between devices, along(): return lax.ppermute(a, axis, [(i, j % n) for i, j in pairs])  20.3 us
    ppermute x10, waiting for transfers between devices, along(): return lax.ppermute(a, axis, [(i, j % n) for i, j in pairs])  14.1 us
    all_to_all x1, blocking collectives, local(): lax.all_to_all(merged, ('y', 'core'), split_axis=0, concat_axis=1, tiled=...  11.8 us
    pallas_call x5, Pallas kernels, attn(): pl.pallas_call(functools.partial(attn_kernel, deltas, blocks, bool(before...  10.2 us
  transfers between devices with their start and end apart: 10, of which 6 were waited for; matrix products, arithmetic and copies ran while one was open for 0% of the time, Pallas kernels for 16%

commit v1 on v0

--- a/solution.py
+++ b/solution.py
@@ -19,14 +19,20 @@
 NEG = -1e30
 PIECE = 2 * TOK + 8
 NEAR = ((0, 0, 0, TOK, 0), (1, 0, 1, TOK, 2), (2, 0, 2, TOK, -2))
-REST = (
+MID = (
     (0, 0, 0, TOK, 1),
     (0, PIECE, 0, PIECE + TOK, 3),
     (1, 0, 1, TOK, -1),
     (1, PIECE, 1, PIECE + TOK, -3),
-    (2, 0, 3, 0, 4),
 )
-EVERY = NEAR + tuple((a + len(NEAR), i, b + len(NEAR), j, shift) for a, i, b, j, shift in REST)
+LAST = ((0, 0, 1, 0, 4),)
+
+
+def moved(blocks, by):
+    return tuple((a + by, i, b + by, j, shift) for a, i, b, j, shift in blocks)
+
+
+EVERY = NEAR + moved(MID, 3) + moved(LAST, 5)
 MIB = 1 << 20
 ROWS = TOK * HEADS
 GROUPS = ROWS // HALF
@@ -278,14 +284,16 @@
     dn13 = along(jnp.concatenate([kv, dn2], axis=0), "z", -1, NZ)
     far_k = along(up2[0:TOK], "z", 2, NZ)
     far_v = along(dn2[TOK:PIECE], "z", -2, NZ)
-    first, rest = [kv, up2, dn2], [up13, dn13, far_k, far_v]
+    first, rest, end = [kv, up2, dn2], [up13, dn13], [far_k, far_v]
     near1 = attn((1,), NEAR, first, [q1], (), "state")
     near2 = attn((2,), NEAR, first, [q2], (), "state")
-    (o1,) = attn((1,), REST, rest, [q1], near1, "send")
+    mid = attn((2, 1), MID, rest, [q2, q1], (*near2, *near1), "state")
+    mid2, mid1 = mid[:3], mid[3:]
+    (o2,) = attn((2,), LAST, end, [q2], mid2, "send")
+    r2 = along(o2, "x", 2, NX)
+    (o1,) = attn((1,), LAST, end, [q1], mid1, "send")
     r1 = along(o1, "x", 1, NX)
-    (o2,) = attn((2,), REST, rest, [q2], near2, "send")
-    r2 = along(o2, "x", 2, NX)
-    o0, lse0 = attn((0,), EVERY, first + rest, [q], (), "keep")
+    o0, lse0 = attn((0,), EVERY, first + rest + end, [q], (), "keep")
     merged = combine(o0, lse0, r1, r2)
     return lax.all_to_all(merged, ("y", "core"), split_axis=0, concat_axis=1, tiled=True)
 

time: 59.2 us -> 62.2 us (1.051)
  the two profiles are of different devices: /device:TPU:4 before, /device:TPU:1 now
where the time goes in v1:
time: 62.2 us; the launch traced here: 61.4 us
  starting transfers between devices  24.3 us (39%)
  waiting for transfers between devices  14 us (23%)
  blocking collectives  13.4 us (22%)
  Pallas kernels  8.84 us (14%)
  local copies, waits for them, and re-layouts  0.73 us (1%)
    ppermute x10, starting transfers between devices, along(): return lax.ppermute(a, axis, [(i, j % n) for i, j in pairs])  24.3 us
    ppermute x10, waiting for transfers between devices, along(): return lax.ppermute(a, axis, [(i, j % n) for i, j in pairs])  14 us
    all_to_all x1, blocking collectives, local(): lax.all_to_all(merged, ('y', 'core'), split_axis=0, concat_axis=1, tiled=...  13.4 us
    pallas_call x6, Pallas kernels, attn(): pl.pallas_call(functools.partial(attn_kernel, deltas, blocks, bool(before...  7.05 us
  transfers between devices with their start and end apart: 10, of which 5 were waited for; matrix products, arithmetic and copies ran while one was open for 0% of the time, Pallas kernels for 10%

profile of v1, /device:TPU:1, one launch (start us, length us, event | category | flops | bytes accessed | tf_op | source)
XLA Modules:
  0.0 61.4 jit_solution(6992654554986191137)
XLA Ops:
  0.0 1.1 %shard_map.46 = (bf16[520,128]{1,0:T(8,128)(2,1)S(1)}, bf16[1032,128]{1,0:T(8,128)(2,1)S(1)}) custom-call(bf16[256,128]{1,0:T(8,128)(2,1)} %bitcast.11, bf16[256,128]{1,0:T(8,128)(2,1)} %bitcast.12, bf16[1024,128]{1,0:T(8,128)(2,1)} %bitcast.10, s32[2,128]{1,0:T(2,128)} %bitcast.13), custom_call_target="tpu_custom_call" | custom-call | tf_op jit(solution)/shard_map/pallas_call | solution.py:68
  1.1 6.9 %collective-permute-start.1 = (bf16[520,128]{1,0:T(8,128)(2,1)S(1)}, bf16[520,128]{1,0:T(8,128)(2,1)S(1)}, u32[]{:S(2)}, u32[]{:S(2)}) collective-permute-start(bf16[520,128]{1,0:T(8,128)(2,1)S(1)} %get-tuple-element.21.refs_0_), channel_id=1, source_target_pairs={{0,48},{8,56},{16,0},{24,8},{32,16},{40,24},{48,32},{56,40},{1,49}... | collective-permute-start | bytes 399368 | tf_op jit(solution)/shard_map/ppermute | solution.py:272
  8.0 0.0 collective-permute-start
  8.0 1.3 %collective-permute-start.7 = (bf16[1032,128]{1,0:T(8,128)(2,1)S(1)}, bf16[1032,128]{1,0:T(8,128)(2,1)S(1)}, u32[]{:S(2)}, u32[]{:S(2)}) collective-permute-start(bf16[1032,128]{1,0:T(8,128)(2,1)S(1)} %get-tuple-element.22.refs_7_), channel_id=1, source_target_pairs={{128,0},{192,64},{129,1},{193,65},{130,2},{194,66},{131,3},{195,67... | collective-permute-start | bytes 792584 | tf_op jit(solution)/shard_map/ppermute | solution.py:272
  9.3 1.3 %collective-permute-start.6 = (bf16[1032,128]{1,0:T(8,128)(2,1)S(1)}, bf16[1032,128]{1,0:T(8,128)(2,1)S(1)}, u32[]{:S(2)}, u32[]{:S(2)}) collective-permute-start(bf16[1032,128]{1,0:T(8,128)(2,1)S(1)} %get-tuple-element.22.refs_7_), channel_id=1, source_target_pairs={{64,0},{128,64},{192,128},{65,1},{129,65},{193,129},{66,2},{130,66... | collective-permute-start | bytes 792584 | tf_op jit(solution)/shard_map/ppermute | solution.py:272
  10.6 0.5 collective-permute-done.1.refs_2_
  11.0 4.3 %collective-permute-done.refs_1_ = bf16[520,128]{1,0:T(8,128)(2,1)S(1)} collective-permute-done((bf16[520,128]{1,0:T(8,128)(2,1)S(1)}, bf16[520,128]{1,0:T(8,128)(2,1)S(1)}, u32[]{:S(2)}, u32[]{:S(2)}) %collective-permute-start) | collective-permute-done | bytes 133152 | tf_op jit(solution)/shard_map/ppermute | solution.py:272
  15.4 0.1 pad_maximum_fusion
  15.4 2.2 %collective-permute-start.3 = (bf16[1040,128]{1,0:T(8,128)(2,1)S(1)}, bf16[1040,128]{1,0:T(8,128)(2,1)S(1)}, u32[]{:S(2)}, u32[]{:S(2)}) collective-permute-start(bf16[1040,128]{1,0:T(8,128)(2,1)S(1)} %get-tuple-element.37), channel_id=1, source_target_pairs={{0,56},{8,0},{16,8},{24,16},{32,24},{40,32},{48,40},{56,48},{1,57}... | collective-permute-start | bytes 798728 | tf_op jit(solution)/shard_map/ppermute | solution.py:272
  17.7 1.0 %collective-permute-start.2 = (bf16[1040,128]{1,0:T(8,128)(2,1)S(1)}, bf16[1040,128]{1,0:T(8,128)(2,1)S(1)}, u32[]{:S(2)}, u32[]{:S(2)}) collective-permute-start(bf16[1040,128]{1,0:T(8,128)(2,1)S(1)} %get-tuple-element.38), channel_id=1, source_target_pairs={{0,8},{8,16},{16,24},{24,32},{32,40},{40,48},{48,56},{56,0},{1,9},... | collective-permute-start | bytes 798728 | tf_op jit(solution)/shard_map/ppermute | solution.py:272
  18.7 0.7 %collective-permute-start.5 = (bf16[264,128]{1,0:T(8,128)(2,1)S(1)}, bf16[264,128]{1,0:T(8,128)(2,1)S(1)}, u32[]{:S(2)}, u32[]{:S(2)}) collective-permute-start(bf16[264,128]{1,0:T(8,128)(2,1)S(1)} %slice.9), channel_id=1, source_target_pairs={{0,48},{8,56},{16,0},{24,8},{32,16},{40,24},{48,32},{56,40},{1,49}... | collective-permute-start | bytes 202760 | tf_op jit(solution)/shard_map/ppermute | solution.py:272
  19.4 0.0 collective-permute-done.6.refs_3_.refs_2_
  19.4 1.7 %collective-permute-start.4 = (bf16[256,128]{1,0:T(8,128)(2,1)S(1)}, bf16[256,128]{1,0:T(8,128)(2,1)S(1)}, u32[]{:S(2)}, u32[]{:S(2)}) collective-permute-start(bf16[256,128]{1,0:T(8,128)(2,1)S(1)} %slice.8), channel_id=1, source_target_pairs={{0,16},{8,24},{16,32},{24,40},{32,48},{40,56},{48,0},{56,8},{1,17}... | collective-permute-start | bytes 196616 | tf_op jit(solution)/shard_map/ppermute | solution.py:272
  21.2 0.6 shard_map.49
  21.8 0.0 collective-permute-done.7.refs_3_.refs_2_
  21.8 0.6 shard_map.48
  22.4 1.2 %collective-permute-done.3.refs_4_.refs_1_ = bf16[1040,128]{1,0:T(8,128)(2,1)S(1)} collective-permute-done((bf16[1040,128]{1,0:T(8,128)(2,1)S(1)}, bf16[1040,128]{1,0:T(8,128)(2,1)S(1)}, u32[]{:S(2)}, u32[]{:S(2)}) %collective-permute-start.3) | collective-permute-done | bytes 266272 | tf_op jit(solution)/shard_map/ppermute | solution.py:272
  23.6 2.6 %collective-permute-done.2.refs_3_.refs_0_ = bf16[1040,128]{1,0:T(8,128)(2,1)S(1)} collective-permute-done((bf16[1040,128]{1,0:T(8,128)(2,1)S(1)}, bf16[1040,128]{1,0:T(8,128)(2,1)S(1)}, u32[]{:S(2)}, u32[]{:S(2)}) %collective-permute-start.2) | collective-permute-done | bytes 266272 | tf_op jit(solution)/shard_map/ppermute | solution.py:272
  26.2 2.1 %shard_map.50 = (f32[1024,128]{1,0:T(8,128)S(1)}, f32[1024,128]{1,0:T(8,128)S(1)}, f32[1024,128]{1,0:T(8,128)S(1)}, f32[1024,128]{1,0:T(8,128)S(1)}, f32[1024,128]{1,0:T(8,128)S(1)}, /*index=5*/f32[1024,128]{1,0:T(8,128)S(1)}) custom-call(bf16[1040,128]{1,0:T(8,128)(2,1)S(1)} %collective-permute-done.2.refs_3_.refs_0_, ...), custom_call_target="tpu_custom_call" | custom-call | flops 1073741824 | bytes 1048576 | tf_op jit(solution)/shard_map/pallas_call | solution.py:206
  28.3 0.0 collective-permute-done.4.refs_5_.refs_0_
  28.3 0.0 collective-permute-done.5.refs_6_.refs_1_
  28.4 0.7 %shard_map.52 = bf16[1048,128]{1,0:T(8,128)(2,1)S(1)} custom-call(bf16[256,128]{1,0:T(8,128)(2,1)S(1)} %collective-permute-done.4.refs_5_.refs_0_, bf16[264,128]{1,0:T(8,128)(2,1)S(1)} %collective-permute-done.5.refs_6_.refs_1_, bf16[1032,128]{1,0:T(8,128)(2,1)S(1)} %collective-permute-done.7.refs_3_.refs_2_, f32[1024,128]{1,0:T(8,128)S(1)} %get-tuple-element.34.refs_3_, ...), custom_call_target="tpu_custom_call" | custom-call | flops 134217728 | bytes 1048576 | tf_op jit(solution)/shard_map/pallas_call | solution.py:206
  29.1 7.7 %collective-permute-start.9 = (bf16[1048,128]{1,0:T(8,128)(2,1)S(1)}, bf16[1048,128]{1,0:T(8,128)(2,1)S(1)}, u32[]{:S(2)}, u32[]{:S(2)}) collective-permute-start(bf16[1048,128]{1,0:T(8,128)(2,1)S(1)} %shard_map.52), channel_id=1, source_target_pairs={{0,128},{64,192},{1,129},{65,193},{2,130},{66,194},{3,131},{67,195... | collective-permute-start | bytes 804872 | tf_op jit(solution)/shard_map/ppermute | solution.py:272
  36.8 0.9 %shard_map.51 = bf16[1048,128]{1,0:T(8,128)(2,1)S(1)} custom-call(bf16[256,128]{1,0:T(8,128)(2,1)S(1)} %collective-permute-done.4.refs_5_.refs_0_, bf16[264,128]{1,0:T(8,128)(2,1)S(1)} %collective-permute-done.5.refs_6_.refs_1_, bf16[1032,128]{1,0:T(8,128)(2,1)S(1)} %collective-permute-done.6.refs_3_.refs_2_, f32[1024,128]{1,0:T(8,128)S(1)} %get-tuple-element.31.refs_3_, ...), custom_call_target="tpu_custom_call" | custom-call | flops 134217728 | bytes 1048576 | tf_op jit(solution)/shard_map/pallas_call | solution.py:206
  37.7 1.3 %collective-permute-start.8 = (bf16[1048,128]{1,0:T(8,128)(2,1)S(1)}, bf16[1048,128]{1,0:T(8,128)(2,1)S(1)}, u32[]{:S(2)}, u32[]{:S(2)}) collective-permute-start(bf16[1048,128]{1,0:T(8,128)(2,1)S(1)} %shard_map.51), channel_id=1, source_target_pairs={{0,64},{64,128},{128,192},{1,65},{65,129},{129,193},{2,66},{66,130... | collective-permute-start | bytes 804872 | tf_op jit(solution)/shard_map/ppermute | solution.py:272
  39.0 2.1 %shard_map.47 = (f32[1024,128]{1,0:T(8,128)S(1)}, f32[8,128]{1,0:T(8,128)S(1)}) custom-call(bf16[520,128]{1,0:T(8,128)(2,1)S(1)} %get-tuple-element.21.refs_0_, bf16[520,128]{1,0:T(8,128)(2,1)S(1)} %collective-permute-done.refs_1_, bf16[520,128]{1,0:T(8,128)(2,1)S(1)} %collective-permute-done.1.refs_2_, ...), custom_call_target="tpu_custom_call" | custom-call | flops 1073741824 | bytes 1048576 | tf_op jit(solution)/shard_map/pallas_call | solution.py:206
  41.2 0.0 collective-permute-done.9.c_ref
  41.2 5.4 %collective-permute-done.8.b_ref = bf16[1048,128]{1,0:T(8,128)(2,1)S(1)} collective-permute-done((bf16[1048,128]{1,0:T(8,128)(2,1)S(1)}, bf16[1048,128]{1,0:T(8,128)(2,1)S(1)}, u32[]{:S(2)}, u32[]{:S(2)}) %collective-permute-start.8) | collective-permute-done | bytes 268320 | tf_op jit(solution)/shard_map/ppermute | solution.py:272
  46.6 0.7 %shard_map.53 = bf16[256,512]{1,0:T(8,128)(2,1)S(1)} custom-call(f32[1024,128]{1,0:T(8,128)S(1)} %get-tuple-element.23.a_ref, f32[8,128]{1,0:T(8,128)S(1)} %get-tuple-element.24.lse_ref, bf16[1048,128]{1,0:T(8,128)(2,1)S(1)} %collective-permute-done.8.b_ref, bf16[1048,128]{1,0:T(8,128)(2,1)S(1)} %collective-permute-done.9.c_ref), custom_call_target="tpu_custom_call" | custom-call | tf_op jit(solution)/shard_map/pallas_call | solution.py:258
  47.3 13.4 %all_to_all.19 = bf16[8,32,512]{2,1,0:T(8,128)(2,1)S(1)} all-to-all(bf16[8,32,512]{2,1,0:T(8,128)(2,1)S(1)} %bitcast.8), channel_id=1, replica_groups=mesh['x'=4,'z'=8,'y'=4,'core'=2] {'y','core'}, dimensions={0} | all-to-all | bytes 524288 | tf_op jit(solution)/shard_map/all_to_all | solution.py:298
  60.7 0.7 %copy.6 = bf16[8,4,8,512]{3,2,0,1:T(8,128)(2,1)} copy(bf16[8,4,8,512]{3,2,1,0:T(8,128)(2,1)S(1)} %bitcast.9) | data formatting | bytes 524288 | tf_op jit(solution)/shard_map/all_to_all | solution.py:298
  (2 shorter events, 0.0 us)
Async XLA Ops:
  1.1 10.0 %collective-permute-start.1 = (bf16[520,128]{1,0:T(8,128)(2,1)S(1)}, bf16[520,128]{1,0:T(8,128)(2,1)S(1)}, u32[]{:S(2)}, u32[]{:S(2)}) collective-permute-start(bf16[520,128]{1,0:T(8,128)(2,1)S(1)} %get-tuple-element.21.refs_0_), channel_id=1, source_target_pairs={{0,48},{8,56},{16,0},{24,8},{32,16},{40,24},{48,32},{56,40},{1,49}... | collective-permute-start | bytes 399368 | tf_op jit(solution)/shard_map/ppermute | solution.py:272
  8.0 7.4 %collective-permute-start = (bf16[520,128]{1,0:T(8,128)(2,1)S(1)}, bf16[520,128]{1,0:T(8,128)(2,1)S(1)}, u32[]{:S(2)}, u32[]{:S(2)}) collective-permute-start(bf16[520,128]{1,0:T(8,128)(2,1)S(1)} %get-tuple-element.21.refs_0_), channel_id=1, source_target_pairs={{0,16},{8,24},{16,32},{24,40},{32,48},{40,56},{48,0},{56,8},{1,17}... | collective-permute-start | bytes 399368 | tf_op jit(solution)/shard_map/ppermute | solution.py:272
  8.0 13.8 %collective-permute-start.7 = (bf16[1032,128]{1,0:T(8,128)(2,1)S(1)}, bf16[1032,128]{1,0:T(8,128)(2,1)S(1)}, u32[]{:S(2)}, u32[]{:S(2)}) collective-permute-start(bf16[1032,128]{1,0:T(8,128)(2,1)S(1)} %get-tuple-element.22.refs_7_), channel_id=1, source_target_pairs={{128,0},{192,64},{129,1},{193,65},{130,2},{194,66},{131,3},{195,67... | collective-permute-start | bytes 792584 | tf_op jit(solution)/shard_map/ppermute | solution.py:272
  9.3 10.1 %collective-permute-start.6 = (bf16[1032,128]{1,0:T(8,128)(2,1)S(1)}, bf16[1032,128]{1,0:T(8,128)(2,1)S(1)}, u32[]{:S(2)}, u32[]{:S(2)}) collective-permute-start(bf16[1032,128]{1,0:T(8,128)(2,1)S(1)} %get-tuple-element.22.refs_7_), channel_id=1, source_target_pairs={{64,0},{128,64},{192,128},{65,1},{129,65},{193,129},{66,2},{130,66... | collective-permute-start | bytes 792584 | tf_op jit(solution)/shard_map/ppermute | solution.py:272
  15.4 8.2 %collective-permute-start.3 = (bf16[1040,128]{1,0:T(8,128)(2,1)S(1)}, bf16[1040,128]{1,0:T(8,128)(2,1)S(1)}, u32[]{:S(2)}, u32[]{:S(2)}) collective-permute-start(bf16[1040,128]{1,0:T(8,128)(2,1)S(1)} %get-tuple-element.37), channel_id=1, source_target_pairs={{0,56},{8,0},{16,8},{24,16},{32,24},{40,32},{48,40},{56,48},{1,57}... | collective-permute-start | bytes 798728 | tf_op jit(solution)/shard_map/ppermute | solution.py:272
  17.7 8.6 %collective-permute-start.2 = (bf16[1040,128]{1,0:T(8,128)(2,1)S(1)}, bf16[1040,128]{1,0:T(8,128)(2,1)S(1)}, u32[]{:S(2)}, u32[]{:S(2)}) collective-permute-start(bf16[1040,128]{1,0:T(8,128)(2,1)S(1)} %get-tuple-element.38), channel_id=1, source_target_pairs={{0,8},{8,16},{16,24},{24,32},{32,40},{40,48},{48,56},{56,0},{1,9},... | collective-permute-start | bytes 798728 | tf_op jit(solution)/shard_map/ppermute | solution.py:272
  18.7 9.6 %collective-permute-start.5 = (bf16[264,128]{1,0:T(8,128)(2,1)S(1)}, bf16[264,128]{1,0:T(8,128)(2,1)S(1)}, u32[]{:S(2)}, u32[]{:S(2)}) collective-permute-start(bf16[264,128]{1,0:T(8,128)(2,1)S(1)} %slice.9), channel_id=1, source_target_pairs={{0,48},{8,56},{16,0},{24,8},{32,16},{40,24},{48,32},{56,40},{1,49}... | collective-permute-start | bytes 202760 | tf_op jit(solution)/shard_map/ppermute | solution.py:272
  19.4 8.9 %collective-permute-start.4 = (bf16[256,128]{1,0:T(8,128)(2,1)S(1)}, bf16[256,128]{1,0:T(8,128)(2,1)S(1)}, u32[]{:S(2)}, u32[]{:S(2)}) collective-permute-start(bf16[256,128]{1,0:T(8,128)(2,1)S(1)} %slice.8), channel_id=1, source_target_pairs={{0,16},{8,24},{16,32},{24,40},{32,48},{40,56},{48,0},{56,8},{1,17}... | collective-permute-start | bytes 196616 | tf_op jit(solution)/shard_map/ppermute | solution.py:272
  29.1 12.1 %collective-permute-start.9 = (bf16[1048,128]{1,0:T(8,128)(2,1)S(1)}, bf16[1048,128]{1,0:T(8,128)(2,1)S(1)}, u32[]{:S(2)}, u32[]{:S(2)}) collective-permute-start(bf16[1048,128]{1,0:T(8,128)(2,1)S(1)} %shard_map.52), channel_id=1, source_target_pairs={{0,128},{64,192},{1,129},{65,193},{2,130},{66,194},{3,131},{67,195... | collective-permute-start | bytes 804872 | tf_op jit(solution)/shard_map/ppermute | solution.py:272
  37.7 8.9 %collective-permute-start.8 = (bf16[1048,128]{1,0:T(8,128)(2,1)S(1)}, bf16[1048,128]{1,0:T(8,128)(2,1)S(1)}, u32[]{:S(2)}, u32[]{:S(2)}) collective-permute-start(bf16[1048,128]{1,0:T(8,128)(2,1)S(1)} %shard_map.51), channel_id=1, source_target_pairs={{0,64},{64,128},{128,192},{1,65},{65,129},{129,193},{2,66},{66,130... | collective-permute-start | bytes 804872 | tf_op jit(solution)/shard_map/ppermute | solution.py:272
